TPU v7x, 128 devices: a whole 4x4x4 slice. The times are simulated.
128 devices in a mesh: row: 16 (over y, z), col: 8 (over x, core).
Axes of the slice: x: 4, y: 4, z: 4, core: 2. Of those that a mesh axis runs over, the one named last changes fastest.
Arguments:
- block_cols: int32 [64, 16], replicated, may hold values from -1 to 63, as said below
- step_dir: bfloat16 [64, 16, 128, 128], P('row', 'col')
- intersection: bfloat16 [64, 16, 128, 128], P('row', 'col')
- density: bfloat16 [64, 16, 128, 128], P('row', 'col')
- kohn_sham: bfloat16 [64, 16, 128, 128], P('row', 'col')
Outputs:
- commutator: bfloat16 [64, 16, 128, 128], P('row', 'col')
- trace_value: float32 [], replicated
Inputs may be any that keep to these rules, and one draw needn't show every extreme that they name: block_cols[i, s] is -1 or a block column of group s // 2, that is from (s // 2) * 8 to (s // 2 + 1) * 8 - 1; the live entries of one block row within one group are distinct; the pattern is symmetric (j is live in row i exactly when i is live in row j) and holds every diagonal block.
All inputs are finite; a program needn't handle non-finite values.
Results may differ from a plain program's by a relative error of at most 0.0057.
Values may be sent and summed in bfloat16 or wider, within the bound.
A program may use at most 64 MiB of HBM per device.

v0:
```python
import jax
import jax.numpy as jnp
from jax import lax
from jax.sharding import PartitionSpec as P


def per_device(block_cols, step_dir, intersection, density, kohn_sham):
    row_total = step_dir.shape[0]
    slot_total = step_dir.shape[1]
    block_size = step_dir.shape[2]
    col_groups = lax.axis_size("col")
    blocks_total = block_cols.shape[0]
    row_index = lax.axis_index("row")
    col_index = lax.axis_index("col")
    own_rows = lax.dynamic_slice_in_dim(block_cols, row_index * row_total, row_total, 0)
    own_cols = lax.dynamic_slice_in_dim(own_rows, col_index * slot_total, slot_total, 1)
    group_cols = lax.dynamic_slice_in_dim(block_cols, col_index * slot_total, slot_total, 1)
    left_live = own_cols >= 0
    targets = own_rows.reshape(row_total, col_groups, slot_total).transpose(1, 0, 2)

    def partial_blocks(left_blocks, gathered, wanted):
        safe_rows = jnp.clip(wanted, 0, blocks_total - 1)
        right_rows = gathered[safe_rows]
        right_cols = group_cols[safe_rows]
        matched = (
            (right_cols[:, :, :, None, :] == own_cols[None, :, None, :, None])
            & left_live[None, :, None, :, None]
            & (wanted >= 0)[:, :, :, None, None]
        )
        picked = jnp.where(
            matched[..., None, None],
            right_rows[:, :, :, None, :, :, :],
            jnp.zeros((), jnp.bfloat16),
        ).sum(axis=4)
        terms = jnp.einsum(
            "iapr,gisaqr->gispq", left_blocks, picked, preferred_element_type=jnp.float32
        )
        group_count = wanted.shape[0]
        return terms.reshape(group_count * row_total, slot_total, block_size, block_size)

    def product(left_blocks, right_blocks):
        gathered = lax.all_gather(right_blocks, "row", axis=0, tiled=True)
        return lax.psum_scatter(
            partial_blocks(left_blocks, gathered, targets), "col", scatter_dimension=0, tiled=True
        )

    scaled_step = product(step_dir, intersection).astype(jnp.bfloat16)
    change = (-(product(scaled_step, density) + product(density, scaled_step))).astype(jnp.bfloat16)
    commutator = (product(kohn_sham, change) - product(change, kohn_sham)).astype(jnp.bfloat16)
    local_trace = jnp.sum(change.astype(jnp.float32) * kohn_sham.astype(jnp.float32))
    trace_value = lax.psum(local_trace, ("row", "col")) / (blocks_total * block_size * block_size)
    return (commutator, trace_value)


def solution(mesh):
    in_specs = (
        P(),
        P("row", "col", None, None),
        P("row", "col", None, None),
        P("row", "col", None, None),
        P("row", "col", None, None),
    )
    out_specs = (P("row", "col", None, None), P())
    return jax.shard_map(
        per_device, mesh=mesh, in_specs=in_specs, out_specs=out_specs, check_vma=False
    )
```

profile of v0, /device:TPU:1, one launch (start us, length us, event | category | flops | bytes accessed | tf_op | source)
XLA Modules:
  0.0 501.8 jit_solution(6847474959793263105)
XLA Ops:
  14.0 50.7 %all-gather.14.cloned.1.call-done = bf16[64,2,128,128]{3,2,1,0:T(8,128)(2,1)} async-done(((bf16[4,2,128,128]{3,2,1,0:T(8,128)(2,1)}), bf16[64,2,128,128]{3,2,1,0:T(8,128)(2,1)}) %all-gather.14.cloned.1.call-update) | async-done | bytes 4194320 | tf_op jit(solution)/shard_map/all_gather | solution.py:42
  64.7 5.2 %gather_fusion.5 = bf16[64,2,128,128]{3,2,1,0:T(8,128)(2,1)} fusion(bf16[64,2,128,128]{3,2,1,0:T(8,128)(2,1)} %all-gather.14.cloned.1.call-done, s32[1024]{0:T(1024)S(1)} %pad_clamp_fusion), kind=kCustom, calls=%fused_computation.5 | custom fusion | bytes 8388864 | tf_op jit(solution)/shard_map/gather | solution.py:23
  69.9 48.0 %all-gather.8.cloned.1.call-done = bf16[64,2,128,128]{3,2,1,0:T(8,128)(2,1)} async-done(((bf16[4,2,128,128]{3,2,1,0:T(8,128)(2,1)}), bf16[64,2,128,128]{3,2,1,0:T(8,128)(2,1)}) %all-gather.8.cloned.1.call-update) | async-done | bytes 4194320 | tf_op jit(solution)/shard_map/all_gather | solution.py:42
  118.0 5.2 %gather_fusion.2 = bf16[64,2,128,128]{3,2,1,0:T(8,128)(2,1)} fusion(bf16[64,2,128,128]{3,2,1,0:T(8,128)(2,1)} %all-gather.8.cloned.1.call-done, s32[1024]{0:T(1024)S(1)} %pad_clamp_fusion), kind=kCustom, calls=%fused_computation.2 | custom fusion | bytes 8388864 | tf_op jit(solution)/shard_map/gather | solution.py:23
  123.2 48.1 %all-gather.6.cloned.1.call-done = bf16[64,2,128,128]{3,2,1,0:T(8,128)(2,1)} async-done(((bf16[4,2,128,128]{3,2,1,0:T(8,128)(2,1)}), bf16[64,2,128,128]{3,2,1,0:T(8,128)(2,1)}) %all-gather.6.cloned.1.call-update) | async-done | bytes 4194320 | tf_op jit(solution)/shard_map/all_gather | solution.py:42
  171.2 5.2 %gather_fusion.1 = bf16[64,2,128,128]{3,2,1,0:T(8,128)(2,1)} fusion(bf16[64,2,128,128]{3,2,1,0:T(8,128)(2,1)} %all-gather.6.cloned.1.call-done, s32[1024]{0:T(1024)S(1)} %pad_clamp_fusion), kind=kCustom, calls=%fused_computation.1 | custom fusion | bytes 8388864 | tf_op jit(solution)/shard_map/gather | solution.py:23
  176.5 17.5 %select_reduce_fusion = (bf16[8,4,2,2,128,128]{5,4,3,2,1,0:T(8,128)(2,1)}, bf16[8,4,2,2,128,128]{5,4,3,2,1,0:T(8,128)(2,1)S(1)}, bf16[8,4,2,2,128,128]{5,4,3,2,1,0:T(8,128)(2,1)}) fusion(pred[8,4,2,2,2]{4,3,2,1,0:T(4,128)(4,1)S(1)} %and_and_fusion, bf16[8,4,2,2,128,128]{5,4,3,2,1,0:T(8,128)(2,1)} %bitcast.70, bf16[8,4,2,2,128,128]{5,4,3,2,1,0:T(8,128)(2,1)} %bitcast.71, ...), kind=kLoop, calls=%fused_computation.6 | loop fusion | flops 18874368 | bytes 25166080 | tf_op jit(solution)/shard_map/reduce_sum | solution.py:34
  193.9 3.2 fusion.11
  197.1 5.4 %copy.48 = f32[8,4,2,128,128]{4,3,2,1,0:T(8,128)} copy(f32[8,4,2,128,128]{3,4,2,0,1:T(8,128)} %fusion.11) | data formatting | bytes 8388608 | tf_op jit(solution)/shard_map/iapr,gisaqr->gispq/transpose | solution.py:35
  202.6 34.9 %reduce-scatter.5.cloned.1.call-done = f32[4,2,128,128]{3,2,1,0:T(8,128)} async-done(((f32[32,2,128,128]{3,2,1,0:T(8,128)}), f32[4,2,128,128]{3,2,1,0:T(8,128)}) %reduce-scatter.5.cloned.1.call-update) | async-done | bytes 524304 | tf_op jit(solution)/shard_map/reduce_scatter | solution.py:43
  239.5 53.7 %all-gather.10.cloned.1.call-done = bf16[64,2,128,128]{3,2,1,0:T(8,128)(2,1)} async-done(((bf16[4,2,128,128]{3,2,1,0:T(8,128)(2,1)}), bf16[64,2,128,128]{3,2,1,0:T(8,128)(2,1)}) %all-gather.10.cloned.1.call-update) | async-done | bytes 4194320 | tf_op jit(solution)/shard_map/all_gather | solution.py:42
  293.2 5.2 %gather_fusion.3 = bf16[64,2,128,128]{3,2,1,0:T(8,128)(2,1)} fusion(bf16[64,2,128,128]{3,2,1,0:T(8,128)(2,1)} %all-gather.10.cloned.1.call-done, s32[1024]{0:T(1024)S(1)} %pad_clamp_fusion), kind=kCustom, calls=%fused_computation.3 | custom fusion | bytes 8388864 | tf_op jit(solution)/shard_map/gather | solution.py:23
  298.4 6.2 %select_reduce_fusion.2 = bf16[8,4,2,2,128,128]{5,4,3,2,1,0:T(8,128)(2,1)S(1)} fusion(pred[8,4,2,2,2]{4,3,2,1,0:T(4,128)(4,1)S(1)} %and_and_fusion, bf16[8,4,2,2,128,128]{5,4,3,2,1,0:T(8,128)(2,1)} %bitcast.69), kind=kLoop, calls=%fused_computation.8 | loop fusion | flops 6291456 | bytes 8388864 | tf_op jit(solution)/shard_map/reduce_sum | solution.py:34
  306.8 3.2 fusion
  310.0 5.4 %copy.51 = f32[8,4,2,128,128]{4,3,2,1,0:T(8,128)} copy(f32[8,4,2,128,128]{3,4,2,0,1:T(8,128)} %fusion) | data formatting | bytes 8388608 | tf_op jit(solution)/shard_map/add | solution.py:48
  315.5 34.8 %reduce-scatter.11.cloned.1.call-done = f32[4,2,128,128]{3,2,1,0:T(8,128)} async-done(((f32[32,2,128,128]{3,2,1,0:T(8,128)}), f32[4,2,128,128]{3,2,1,0:T(8,128)}) %reduce-scatter.11.cloned.1.call-update) | async-done | bytes 524304 | tf_op jit(solution)/shard_map/reduce_scatter | solution.py:43
  352.8 5.4 %fusion.17 = f32[8,4,2,128,128]{3,4,2,0,1:T(8,128)} fusion(bf16[8,4,2,2,128,128]{5,4,3,2,1,0:T(8,128)(2,1)} %get-tuple-element.2, bf16[4,2,128,128]{3,2,1,0:T(8,128)(2,1)} %get-tuple-element.6), kind=kOutput, calls=%fused_computation.25 | convolution fusion | flops 536870912 | bytes 8650752 | tf_op jit(solution)/shard_map/iapr,gisaqr->gispq/dot_general | solution.py:35
  358.2 5.4 %copy.55 = f32[8,4,2,128,128]{4,3,2,1,0:T(8,128)} copy(f32[8,4,2,128,128]{3,4,2,0,1:T(8,128)} %fusion.17) | data formatting | bytes 8388608 | tf_op jit(solution)/shard_map/iapr,gisaqr->gispq/transpose | solution.py:35
  363.6 42.6 %all-gather.12.cloned.1.call-done = bf16[64,2,128,128]{3,2,1,0:T(8,128)(2,1)} async-done(((bf16[4,2,128,128]{3,2,1,0:T(8,128)(2,1)}), bf16[64,2,128,128]{3,2,1,0:T(8,128)(2,1)}) %all-gather.12.cloned.1.call-update) | async-done | bytes 4194320 | tf_op jit(solution)/shard_map/all_gather | solution.py:42
  406.2 5.2 %gather_fusion.4 = bf16[64,2,128,128]{3,2,1,0:T(8,128)(2,1)} fusion(bf16[64,2,128,128]{3,2,1,0:T(8,128)(2,1)} %all-gather.12.cloned.1.call-done, s32[1024]{0:T(1024)S(1)} %pad_clamp_fusion), kind=kCustom, calls=%fused_computation.4 | custom fusion | bytes 8388864 | tf_op jit(solution)/shard_map/gather | solution.py:23
  411.5 6.2 %select_reduce_fusion.1 = bf16[8,4,2,2,128,128]{5,4,3,2,1,0:T(8,128)(2,1)S(1)} fusion(pred[8,4,2,2,2]{4,3,2,1,0:T(4,128)(4,1)S(1)} %and_and_fusion, bf16[8,4,2,2,128,128]{5,4,3,2,1,0:T(8,128)(2,1)} %bitcast.68), kind=kLoop, calls=%fused_computation.7 | loop fusion | flops 6291456 | bytes 8388864 | tf_op jit(solution)/shard_map/reduce_sum | solution.py:34
  417.6 3.2 fusion.14
  420.8 5.5 %copy.53 = f32[8,4,2,128,128]{4,3,2,1,0:T(8,128)} copy(f32[8,4,2,128,128]{3,4,2,0,1:T(8,128)} %fusion.14) | data formatting | bytes 8388608 | tf_op jit(solution)/shard_map/iapr,gisaqr->gispq/transpose | solution.py:35
  426.4 65.1 %psum.7 = f32[]{:T(128)} all-reduce(f32[]{:T(128)} %get-tuple-element.5), channel_id=1, replica_groups=mesh['row'=16,'col'=8] {'row','col'}, use_global_device_ids=true, to_apply=%region_11.12 | all-reduce | flops 1 | bytes 8 | tf_op jit(solution)/shard_map/psum | solution.py:51
  (52 shorter events, 15.6 us)
Async XLA Ops:
  7.2 186.8 %copy-start = (bf16[4,2,128,128]{3,2,1,0:T(8,128)(2,1)S(1)}, bf16[4,2,128,128]{3,2,1,0:T(8,128)(2,1)}, u32[]{:S(2)}) copy-start(bf16[4,2,128,128]{3,2,1,0:T(8,128)(2,1)} %param.6) | copy-start | bytes 786436
  7.2 57.5 %all-gather.14.cloned.1.call-start = ((), (), s32[]{:S(2)}) async-start(), calls=%async_computation.10 | async-start | bytes 4456448 | tf_op jit(solution)/shard_map/all_gather | solution.py:42
  7.9 110.1 %all-gather.8.cloned.1.call-start = ((), (), s32[]{:S(2)}) async-start(), calls=%async_computation.5 | async-start | bytes 4456448 | tf_op jit(solution)/shard_map/all_gather | solution.py:42
  8.7 162.6 %all-gather.6.cloned.1.call-start = ((), (), s32[]{:S(2)}) async-start(), calls=%async_computation.4 | async-start | bytes 4456448 | tf_op jit(solution)/shard_map/all_gather | solution.py:42
  9.4 228.0 %reduce-scatter.5.cloned.1.call-start = ((), (), s32[]{:S(2)}) async-start(), calls=%async_computation.6 | async-start | bytes 4718592 | tf_op jit(solution)/shard_map/reduce_scatter | solution.py:43
  202.5 90.7 %all-gather.10.cloned.1.call-start = ((), (), s32[]{:S(2)}) async-start(), calls=%async_computation.7 | async-start | bytes 4456448 | tf_op jit(solution)/shard_map/all_gather | solution.py:42
  239.2 111.0 %reduce-scatter.11.cloned.1.call-start = ((), (), s32[]{:S(2)}) async-start(), calls=%async_computation.12 | async-start | bytes 4718592 | tf_op jit(solution)/shard_map/reduce_scatter | solution.py:43
  298.4 6.2 %copy-start.4 = (bf16[4,2,128,128]{3,2,1,0:T(8,128)(2,1)S(1)}, bf16[4,2,128,128]{3,2,1,0:T(8,128)(2,1)}, u32[]{:S(2)}) copy-start(bf16[4,2,128,128]{3,2,1,0:T(8,128)(2,1)} %param.8) | copy-start | bytes 786436
  304.6 2.2 copy-start.2
  304.6 2.2 copy-start.3
  315.4 34.9 %copy-start.5 = (bf16[4,2,128,128]{3,2,1,0:T(8,128)(2,1)S(1)}, bf16[4,2,128,128]{3,2,1,0:T(8,128)(2,1)}, u32[]{:S(2)}) copy-start(bf16[4,2,128,128]{3,2,1,0:T(8,128)(2,1)} %param.9) | copy-start | bytes 786436
  315.4 90.8 %all-gather.12.cloned.1.call-start = ((), (), s32[]{:S(2)}) async-start(), calls=%async_computation.8 | async-start | bytes 4456448 | tf_op jit(solution)/shard_map/all_gather | solution.py:42
  352.7 139.4 %reduce-scatter.9.cloned.1.call-start = ((), (), s32[]{:S(2)}) async-start(), calls=%async_computation.11 | async-start | bytes 4718592 | tf_op jit(solution)/shard_map/reduce_scatter | solution.py:43
  363.6 128.6 %reduce-scatter.7.cloned.1.call-start = ((), (), s32[]{:S(2)}) async-start(), calls=%async_computation.9 | async-start | bytes 4718592 | tf_op jit(solution)/shard_map/reduce_scatter | solution.py:43
  420.8 73.3 %copy-start.1 = (bf16[4,2,128,128]{3,2,1,0:T(8,128)(2,1)S(1)}, bf16[4,2,128,128]{3,2,1,0:T(8,128)(2,1)}, u32[]{:S(2)}) copy-start(bf16[4,2,128,128]{3,2,1,0:T(8,128)(2,1)} %param.6) | copy-start | bytes 786436
Sparse Core Ops, SparseCore 0:
  10.1 54.5 all-gather.13
  66.8 51.0 all-gather.7
  120.1 51.0 all-gather.5
  202.6 34.7 reduce-scatter.4
  240.0 53.1 all-gather.9
  315.5 34.6 reduce-scatter.10
  353.0 53.2 all-gather.11
  408.6 35.0 reduce-scatter.8
  446.1 37.3 reduce-scatter.6
where the time goes:
time: 503 us; the launch traced here: 502 us
  waiting for transfers between devices  315 us (63%)
  blocking collectives  65.1 us (13%)
  local copies, waits for them, and re-layouts  50.7 us (10%)
  other arithmetic  38.5 us (8%)
  matrix products  16.3 us (3%)
  between operations  15.7 us (3%)
    all_gather x5, waiting for transfers between devices, product(): gathered = lax.all_gather(right_blocks, 'row', axis=0, tiled=True)  243 us
    reduce_scatter x4, waiting for transfers between devices, product(): lax.psum_scatter(partial_blocks(left_blocks, gathered, targets), 'col', s...  69.7 us
    psum x1, blocking collectives, per_device(): lax.psum(local_trace, ('row', 'col'))  65.1 us
    reduce_sum x3, other arithmetic, partial_blocks(): picked = jnp.where(matched[..., None, None], right_rows[:, :, :, None, :,...  29.8 us
    gather x5, local copies, waits for them, and re-layouts, partial_blocks(): right_rows = gathered[safe_rows]  26.1 us
    dot_general x5, matrix products, partial_blocks(): jnp.einsum('iapr,gisaqr->gispq', left_blocks, picked, preferred_element_t...  16.3 us
    transpose x3, local copies, waits for them, and re-layouts, partial_blocks(): jnp.einsum('iapr,gisaqr->gispq', left_blocks, picked, preferred_element_t...  16.2 us
  transfers between devices with their start and end apart: 9, of which 7 were waited for; matrix products, arithmetic and copies ran while one was open for 9% of the time, Pallas kernels for 0%

commit v1 on v0

--- a/solution.py
+++ b/solution.py
@@ -2,6 +2,13 @@
 import jax.numpy as jnp
 from jax import lax
 from jax.sharding import PartitionSpec as P
+
+
+def all_by_exchange(x, axis, dim):
+    devices = lax.axis_size(axis)
+    parts = jnp.stack([x for _ in range(devices)])
+    parts = lax.all_to_all(parts, axis, split_axis=0, concat_axis=0)
+    return jnp.concatenate(parts, axis=dim)
 
 
 def per_device(block_cols, step_dir, intersection, density, kohn_sham):
@@ -39,7 +46,7 @@
         return terms.reshape(group_count * row_total, slot_total, block_size, block_size)
 
     def product(left_blocks, right_blocks):
-        gathered = lax.all_gather(right_blocks, "row", axis=0, tiled=True)
+        gathered = all_by_exchange(right_blocks, "row", 0)
         return lax.psum_scatter(
             partial_blocks(left_blocks, gathered, targets), "col", scatter_dimension=0, tiled=True
         )

time: 503 us -> 533 us (1.060)
  blocking collectives: 65.1 us -> 287 us
  waiting for transfers between devices: 315 us -> 114 us
  local copies, waits for them, and re-layouts: 50.7 us -> 58 us
    all_gather x5 -> x0, waiting for transfers between devices: 243 us -> none  [product(): gathered = lax.all_gather(right_blocks, 'row', axis=0, tiled=True)]
    all_to_all x0 -> x4, blocking collectives: none -> 217 us  [all_by_exchange(): parts = lax.all_to_all(parts, axis, split_axis=0, concat_axis=0)]
    all_to_all x0 -> x1, waiting for transfers between devices: none -> 36.6 us  [all_by_exchange(): parts = lax.all_to_all(parts, axis, split_axis=0, concat_axis=0)]
    another operation x0 -> x5, local copies, waits for them, and re-layouts: none -> 8.15 us  [all_by_exchange(): parts = jnp.stack([x for _ in range(devices)])]
    reduce_scatter x4, waiting for transfers between devices: 69.7 us -> 77.8 us  [product(): lax.psum_scatter(partial_blocks(left_blocks, gathered, targets), 'col', s...]
  transfers between devices with their start and end apart: 9 -> 5, of which waited for: 7 -> 3; matrix products, arithmetic and copies ran while one was open for 9% -> 6% of each run, Pallas kernels for 0% -> 0%
where the time goes in v1:
time: 533 us; the launch traced here: 532 us
  blocking collectives  287 us (54%)
  waiting for transfers between devices  114 us (21%)
  local copies, waits for them, and re-layouts  58 us (11%)
  other arithmetic  35 us (7%)
  matrix products  16.3 us (3%)
  between operations  15.7 us (3%)
    all_to_all x4, blocking collectives, all_by_exchange(): parts = lax.all_to_all(parts, axis, split_axis=0, concat_axis=0)  217 us
    reduce_scatter x4, waiting for transfers between devices, product(): lax.psum_scatter(partial_blocks(left_blocks, gathered, targets), 'col', s...  77.8 us
    psum x1, blocking collectives, per_device(): lax.psum(local_trace, ('row', 'col'))  70.1 us
    all_to_all x1, waiting for transfers between devices, all_by_exchange(): parts = lax.all_to_all(parts, axis, split_axis=0, concat_axis=0)  36.6 us
    reduce_sum x3, other arithmetic, partial_blocks(): picked = jnp.where(matched[..., None, None], right_rows[:, :, :, None, :,...  29.8 us
    gather x5, local copies, waits for them, and re-layouts, partial_blocks(): right_rows = gathered[safe_rows]  26.1 us
    dot_general x5, matrix products, partial_blocks(): jnp.einsum('iapr,gisaqr->gispq', left_blocks, picked, preferred_element_t...  16.3 us
    transpose x3, local copies, waits for them, and re-layouts, partial_blocks(): jnp.einsum('iapr,gisaqr->gispq', left_blocks, picked, preferred_element_t...  16.1 us
  transfers between devices with their start and end apart: 5, of which 3 were waited for; matrix products, arithmetic and copies ran while one was open for 6% of the time, Pallas kernels for 0%

profile of v1, /device:TPU:1, one launch (start us, length us, event | category | flops | bytes accessed | tf_op | source)
XLA Modules:
  0.0 531.6 jit_solution(13677061195934914535)
XLA Ops:
  9.2 57.9 %all_to_all.25 = bf16[16,4,2,128,128]{4,3,2,1,0:T(8,128)(2,1)} all-to-all(bf16[16,4,2,128,128]{4,3,2,1,0:T(8,128)(2,1)S(1)} %stack.11), channel_id=1, replica_groups=mesh['row'=16,'col'=8] {'row'}, dimensions={0} | all-to-all | bytes 8388608 | tf_op jit(solution)/shard_map/all_to_all | solution.py:10
  68.2 53.3 %all_to_all.26 = bf16[16,4,2,128,128]{4,3,2,1,0:T(8,128)(2,1)} all-to-all(bf16[16,4,2,128,128]{4,3,2,1,0:T(8,128)(2,1)S(1)} %stack.10), channel_id=1, replica_groups=mesh['row'=16,'col'=8] {'row'}, dimensions={0} | all-to-all | bytes 8388608 | tf_op jit(solution)/shard_map/all_to_all | solution.py:10
  124.5 4.7 all-to-all-start.4
  131.2 5.2 gather_fusion.2
  136.4 5.2 gather_fusion.1
  141.7 36.6 %all-to-all-done.4 = bf16[16,4,2,128,128]{4,3,2,1,0:T(8,128)(2,1)} async-done(((bf16[16,4,2,128,128]{4,3,2,1,0:T(8,128)(2,1)}), bf16[16,4,2,128,128]{4,3,2,1,0:T(8,128)(2,1)}, u32[]{:S(2)}, u32[]{:S(2)}) %all-to-all-start.4) | async-done | bytes 4194336 | tf_op jit(solution)/shard_map/all_to_all | solution.py:10
  178.2 5.2 gather_fusion.5
  183.4 17.5 %select_reduce_fusion = (bf16[8,4,2,2,128,128]{5,4,3,2,1,0:T(8,128)(2,1)}, bf16[8,4,2,2,128,128]{5,4,3,2,1,0:T(8,128)(2,1)S(1)}, bf16[8,4,2,2,128,128]{5,4,3,2,1,0:T(8,128)(2,1)}) fusion(pred[8,4,2,2,2]{4,3,2,1,0:T(4,128)(4,1)S(1)} %and_and_fusion, bf16[8,4,2,2,128,128]{5,4,3,2,1,0:T(8,128)(2,1)} %bitcast.81, bf16[8,4,2,2,128,128]{5,4,3,2,1,0:T(8,128)(2,1)} %bitcast.79, ...), kind=kLoop, calls=%fused_computation.6 | loop fusion | flops 18874368 | bytes 25166080 | tf_op jit(solution)/shard_map/reduce_sum | solution.py:41
  204.1 5.3 %copy.36 = f32[8,4,2,128,128]{4,3,2,1,0:T(8,128)} copy(f32[8,4,2,128,128]{3,4,2,0,1:T(8,128)} %fusion.11) | data formatting | bytes 8388608 | tf_op jit(solution)/shard_map/iapr,gisaqr->gispq/transpose | solution.py:42
  209.6 39.8 %reduce-scatter.5.cloned.1.call-done = f32[4,2,128,128]{3,2,1,0:T(8,128)} async-done(((f32[32,2,128,128]{3,2,1,0:T(8,128)}), f32[4,2,128,128]{3,2,1,0:T(8,128)}) %reduce-scatter.5.cloned.1.call-update) | async-done | bytes 524304 | tf_op jit(solution)/shard_map/reduce_scatter | solution.py:50
  251.5 52.9 %all_to_all.27 = bf16[16,4,2,128,128]{4,3,2,1,0:T(8,128)(2,1)} all-to-all(bf16[16,4,2,128,128]{4,3,2,1,0:T(8,128)(2,1)S(1)} %stack.12), channel_id=1, replica_groups=mesh['row'=16,'col'=8] {'row'}, dimensions={0} | all-to-all | bytes 8388608 | tf_op jit(solution)/shard_map/all_to_all | solution.py:10
  304.4 5.2 gather_fusion.3
  309.7 6.2 %select_reduce_fusion.2 = bf16[8,4,2,2,128,128]{5,4,3,2,1,0:T(8,128)(2,1)S(1)} fusion(pred[8,4,2,2,2]{4,3,2,1,0:T(4,128)(4,1)S(1)} %and_and_fusion, bf16[8,4,2,2,128,128]{5,4,3,2,1,0:T(8,128)(2,1)} %bitcast.78), kind=kLoop, calls=%fused_computation.8 | loop fusion | flops 6291456 | bytes 8388864 | tf_op jit(solution)/shard_map/reduce_sum | solution.py:41
  318.0 3.2 fusion
  321.2 5.3 %copy.39 = f32[8,4,2,128,128]{4,3,2,1,0:T(8,128)} copy(f32[8,4,2,128,128]{3,4,2,0,1:T(8,128)} %fusion) | data formatting | bytes 8388608 | tf_op jit(solution)/shard_map/add | solution.py:55
  326.7 37.9 %reduce-scatter.11.cloned.1.call-done = f32[4,2,128,128]{3,2,1,0:T(8,128)} async-done(((f32[32,2,128,128]{3,2,1,0:T(8,128)}), f32[4,2,128,128]{3,2,1,0:T(8,128)}) %reduce-scatter.11.cloned.1.call-update) | async-done | bytes 524304 | tf_op jit(solution)/shard_map/reduce_scatter | solution.py:50
  366.3 5.4 %fusion.17 = f32[8,4,2,128,128]{3,4,2,0,1:T(8,128)} fusion(bf16[8,4,2,2,128,128]{5,4,3,2,1,0:T(8,128)(2,1)} %get-tuple-element.2, bf16[4,2,128,128]{3,2,1,0:T(8,128)(2,1)S(1)} %get-tuple-element.6), kind=kOutput, calls=%fused_computation.25 | convolution fusion | flops 536870912 | bytes 8650752 | tf_op jit(solution)/shard_map/iapr,gisaqr->gispq/dot_general | solution.py:42
  371.8 5.4 %copy.43 = f32[8,4,2,128,128]{4,3,2,1,0:T(8,128)} copy(f32[8,4,2,128,128]{3,4,2,0,1:T(8,128)} %fusion.17) | data formatting | bytes 8388608 | tf_op jit(solution)/shard_map/iapr,gisaqr->gispq/transpose | solution.py:42
  378.2 53.0 %all_to_all.28 = bf16[16,4,2,128,128]{4,3,2,1,0:T(8,128)(2,1)} all-to-all(bf16[16,4,2,128,128]{4,3,2,1,0:T(8,128)(2,1)S(1)} %stack.13), channel_id=1, replica_groups=mesh['row'=16,'col'=8] {'row'}, dimensions={0} | all-to-all | bytes 8388608 | tf_op jit(solution)/shard_map/all_to_all | solution.py:10
  431.2 5.2 gather_fusion.4
  436.4 6.2 %select_reduce_fusion.1 = bf16[8,4,2,2,128,128]{5,4,3,2,1,0:T(8,128)(2,1)S(1)} fusion(pred[8,4,2,2,2]{4,3,2,1,0:T(4,128)(4,1)S(1)} %and_and_fusion, bf16[8,4,2,2,128,128]{5,4,3,2,1,0:T(8,128)(2,1)} %bitcast.75), kind=kLoop, calls=%fused_computation.7 | loop fusion | flops 6291456 | bytes 8388864 | tf_op jit(solution)/shard_map/reduce_sum | solution.py:41
  442.6 3.2 fusion.14
  445.8 5.4 %copy.41 = f32[8,4,2,128,128]{4,3,2,1,0:T(8,128)} copy(f32[8,4,2,128,128]{3,4,2,0,1:T(8,128)} %fusion.14) | data formatting | bytes 8388608 | tf_op jit(solution)/shard_map/iapr,gisaqr->gispq/transpose | solution.py:42
  451.3 70.1 %psum.7 = f32[]{:T(128)} all-reduce(f32[]{:T(128)} %get-tuple-element.5), channel_id=1, replica_groups=mesh['row'=16,'col'=8] {'row','col'}, use_global_device_ids=true, to_apply=%region_11.12 | all-reduce | flops 1 | bytes 8 | tf_op jit(solution)/shard_map/psum | solution.py:58
  (48 shorter events, 20.6 us)
Async XLA Ops:
  7.2 193.8 %copy-start = (bf16[4,2,128,128]{3,2,1,0:T(8,128)(2,1)S(1)}, bf16[4,2,128,128]{3,2,1,0:T(8,128)(2,1)}, u32[]{:S(2)}) copy-start(bf16[4,2,128,128]{3,2,1,0:T(8,128)(2,1)} %param.6) | copy-start | bytes 786436
  9.2 57.9 %copy-start.3 = (bf16[4,2,128,128]{3,2,1,0:T(8,128)(2,1)S(1)}, bf16[4,2,128,128]{3,2,1,0:T(8,128)(2,1)}, u32[]{:S(2)}) copy-start(bf16[4,2,128,128]{3,2,1,0:T(8,128)(2,1)} %param.8) | copy-start | bytes 786436
  68.2 53.3 %copy-start.4 = (bf16[4,2,128,128]{3,2,1,0:T(8,128)(2,1)S(1)}, bf16[4,2,128,128]{3,2,1,0:T(8,128)(2,1)}, u32[]{:S(2)}) copy-start(bf16[4,2,128,128]{3,2,1,0:T(8,128)(2,1)} %param.9) | copy-start | bytes 786436
  124.5 4.9 copy-start.5
  124.5 53.8 %all-to-all-start.4 = ((bf16[16,4,2,128,128]{4,3,2,1,0:T(8,128)(2,1)}), bf16[16,4,2,128,128]{4,3,2,1,0:T(8,128)(2,1)}, u32[]{:S(2)}, u32[]{:S(2)}) async-start(bf16[16,4,2,128,128]{4,3,2,1,0:T(8,128)(2,1)} %stack.14), calls=%async_computation.6 | async-start | bytes 8388608 | tf_op jit(solution)/shard_map/all_to_all | solution.py:10
  129.2 120.2 %reduce-scatter.5.cloned.1.call-start = ((), (), s32[]{:S(2)}) async-start(), calls=%async_computation.9 | async-start | bytes 4718592 | tf_op jit(solution)/shard_map/reduce_scatter | solution.py:50
  209.5 155.0 %reduce-scatter.11.cloned.1.call-start = ((), (), s32[]{:S(2)}) async-start(), calls=%async_computation.12 | async-start | bytes 4718592 | tf_op jit(solution)/shard_map/reduce_scatter | solution.py:50
  315.8 2.2 copy-start.2
  326.6 195.4 %reduce-scatter.9.cloned.1.call-start = ((), (), s32[]{:S(2)}) async-start(), calls=%async_computation.11 | async-start | bytes 4718592 | tf_op jit(solution)/shard_map/reduce_scatter | solution.py:50
  377.1 144.9 %reduce-scatter.7.cloned.1.call-start = ((), (), s32[]{:S(2)}) async-start(), calls=%async_computation.10 | async-start | bytes 4718592 | tf_op jit(solution)/shard_map/reduce_scatter | solution.py:50
  445.8 78.1 %copy-start.1 = (bf16[4,2,128,128]{3,2,1,0:T(8,128)(2,1)S(1)}, bf16[4,2,128,128]{3,2,1,0:T(8,128)(2,1)}, u32[]{:S(2)}) copy-start(bf16[4,2,128,128]{3,2,1,0:T(8,128)(2,1)} %param.6) | copy-start | bytes 786436
Sparse Core Ops, SparseCore 0:
  209.6 39.7 reduce-scatter.4
  326.7 37.7 reduce-scatter.10
  377.3 37.4 reduce-scatter.8
  451.4 38.3 reduce-scatter.6
